TPU v7x, 32 devices: a whole 2x2x4 slice. The times are simulated.
32 devices in a mesh: gx: 4 (over y, core), gy: 8 (over z, x).
Axes of the slice: x: 2, y: 2, z: 4, core: 2. Of those that a mesh axis runs over, the one named last changes fastest.
Arguments:
- forcing: float32 [2, 20, 64, 1024], P(None, None, 'gx', 'gy'), may hold values from -6 to 6
- viscosity: float32 [20, 64, 1024], P(None, 'gx', 'gy'), may hold values from 0.5 to 8
- spread: float32 [20, 64, 1024], P(None, 'gx', 'gy'), may hold values from 0.2 to 2
- coupling: float32 [64, 1024], P('gx', 'gy'), may hold values from -0.5 to 0.5
- friction: float32 [64, 1024], P('gx', 'gy'), may hold values from 0.05 to 5
- ice_mask: int32 [64, 1024], P('gx', 'gy'), may hold values 0 or 1
- aggregates: int32 [64, 1024], P('gx', 'gy'), may hold values from 0 to 127, as said below
Outputs:
- solution: float32 [2, 20, 64, 1024], P(None, None, 'gx', 'gy')
- residual: float32 [2, 20, 64, 1024], P(None, None, 'gx', 'gy')
Inputs may be any that keep to these rules, and one draw needn't show every extreme that they name: `aggregates`: within each device block of 16 x 128 columns, every number from 0 to 127 names some columns of that block.
All inputs are finite; a program needn't handle non-finite values. No bound on the sum of `ice_mask` on one device may be relied on, other than what follows from the above.
Results may differ from a plain program's by a relative error of at most 0.0013.
Values sent between devices are 32-bit elements; how exact they have to be, the bound alone decides.
A program may use at most 128 MiB of HBM per device.

v0:
```python
import jax
import jax.numpy as jnp
from jax import lax
from jax.sharding import PartitionSpec as P

ITERS = 3
SWEEPS = 2
CSWEEPS = 4


LINE_WEIGHT = 0.8
POINT_WEIGHT = 0.7
COARSE_WEIGHT = 0.7


def extended(cells, sides, width):
    for axis, dim in sides:
        count = lax.axis_size(axis)
        ends = count - 1
        head = lax.slice_in_dim(cells, 0, width, axis=dim)
        tail = lax.slice_in_dim(cells, cells.shape[dim] - width, cells.shape[dim], axis=dim)
        cells = jnp.concatenate(
            [
                lax.ppermute(tail, axis, [(i, (i + 1) % count) for i in range(ends)]),
                cells,
                lax.ppermute(head, axis, [((i + 1) % count, i) for i in range(ends)]),
            ],
            axis=dim,
        )
    return cells


def beside_all(padded):
    return (
        padded[..., 2:, 1:-1],
        padded[..., :-2, 1:-1],
        padded[..., 1:-1, 2:],
        padded[..., 1:-1, :-2],
    )


def fine_coefficients(viscosity, spread, coupling, friction, ice_float, mask_padded):
    east_mask, west_mask, north_mask, south_mask = beside_all(mask_padded)
    vertical = 0.5 * (viscosity[:-1] + viscosity[1:]) * ice_float
    face_total = jnp.pad(vertical, ((0, 1), (0, 0), (0, 0))) + jnp.pad(
        vertical, ((1, 0), (0, 0), (0, 0))
    )
    bottom = jnp.pad(friction[None], ((0, viscosity.shape[0] - 1), (0, 0), (0, 0)))
    diagonal = ice_float * (face_total + 4.0 * spread + bottom) + (1.0 - ice_float)
    owned_spread = spread * ice_float
    return (
        diagonal,
        vertical,
        owned_spread * east_mask,
        owned_spread * west_mask,
        owned_spread * north_mask,
        owned_spread * south_mask,
        bottom * coupling * ice_float,
    )


def group_layers(level_coefs, group_size):
    diagonal, vertical, to_east, to_west, to_north, to_south, crossed = level_coefs
    group_count = diagonal.shape[0] // group_size

    def fold_layers(values):
        return values.reshape((group_count, group_size) + values.shape[1:]).sum(axis=1)

    padded = jnp.concatenate([vertical, jnp.zeros_like(diagonal[:1])], axis=0)
    blocks = padded.reshape((group_count, group_size) + padded.shape[1:])
    inner_sum = blocks[:, : group_size - 1].sum(axis=1)
    return (
        fold_layers(diagonal) - 2.0 * inner_sum,
        blocks[:-1, group_size - 1],
        fold_layers(to_east),
        fold_layers(to_west),
        fold_layers(to_north),
        fold_layers(to_south),
        fold_layers(crossed),
    )


def apply_stencil(level_coefs, grid_field, padded):
    diagonal, vertical, to_east, to_west, to_north, to_south, crossed = level_coefs
    east_value, west_value, north_value, south_value = beside_all(padded)
    result = (
        diagonal * grid_field
        + crossed * grid_field[::-1]
        - (
            to_east * east_value
            + to_west * west_value
            + to_north * north_value
            + to_south * south_value
        )
    )
    if vertical.shape[0] > 0:
        upward = vertical * grid_field[:, 1:]
        downward = vertical * grid_field[:, :-1]
        result = result - (
            jnp.pad(upward, ((0, 0), (0, 1), (0, 0), (0, 0)))
            + jnp.pad(downward, ((0, 0), (1, 0), (0, 0), (0, 0)))
        )
    return result


def line_factor(level_coefs):
    diagonal, vertical = (level_coefs[0], level_coefs[1])
    inverse = [1.0 / diagonal[0]]
    upper = []
    for layer_at in range(1, diagonal.shape[0]):
        ratio_value = -vertical[layer_at - 1] * inverse[-1]
        upper.append(ratio_value)
        inverse.append(1.0 / (diagonal[layer_at] + vertical[layer_at - 1] * ratio_value))
    return (inverse, upper, vertical)


def line_solve(factor, right_side):
    inverse, upper, vertical = factor
    layers = len(inverse)
    forward = [right_side[:, 0] * inverse[0]]
    for layer_at in range(1, layers):
        forward.append(
            (right_side[:, layer_at] + vertical[layer_at - 1] * forward[-1]) * inverse[layer_at]
        )
    backward = [forward[-1]]
    for layer_at in range(layers - 2, -1, -1):
        backward.append(forward[layer_at] - upper[layer_at] * backward[-1])
    return jnp.stack(backward[::-1], axis=1)


def group_sum(grid_field, group_size):
    return grid_field.reshape(
        (2, grid_field.shape[1] // group_size, group_size) + grid_field.shape[2:]
    ).sum(axis=2)


def expand_layers(grid_field, group_size):
    return jnp.repeat(grid_field, group_size, axis=1)


def point_diagonal(column_coefs, group_ids, group_count):
    ids_padded = jnp.pad(group_ids, 1, constant_values=-1)
    east_id, west_id, north_id, south_id = beside_all(ids_padded)
    inner_sum = (
        jnp.where(east_id == group_ids, column_coefs[2][0], 0.0)
        + jnp.where(west_id == group_ids, column_coefs[3][0], 0.0)
        + jnp.where(north_id == group_ids, column_coefs[4][0], 0.0)
        + jnp.where(south_id == group_ids, column_coefs[5][0], 0.0)
    )
    return jax.ops.segment_sum(
        (column_coefs[0][0] - inner_sum).reshape(-1),
        group_ids.reshape(-1),
        num_segments=group_count,
    )


def coarse_coefficients(column_coefs, blocks_first, blocks_second):
    diagonal, vertical, to_east, to_west, to_north, to_south, crossed = column_coefs

    def split_block(values):
        plane = values[0]
        return plane.reshape(
            blocks_first,
            plane.shape[0] // blocks_first,
            blocks_second,
            plane.shape[1] // blocks_second,
        )

    east_block = split_block(to_east)
    west_block = split_block(to_west)
    north_block = split_block(to_north)
    south_block = split_block(to_south)
    inner_sum = (
        east_block[:, :-1].sum(axis=(1, 3))
        + west_block[:, 1:].sum(axis=(1, 3))
        + north_block[:, :, :, :-1].sum(axis=(1, 3))
        + south_block[:, :, :, 1:].sum(axis=(1, 3))
    )
    return (
        split_block(diagonal).sum(axis=(1, 3)) - inner_sum,
        split_block(crossed).sum(axis=(1, 3)),
        east_block[:, -1].sum(axis=2),
        west_block[:, 0].sum(axis=2),
        north_block[:, :, :, -1].sum(axis=1),
        south_block[:, :, :, 0].sum(axis=1),
    )


def coarse_apply(block_table, grid_field, padded):
    diagonal, crossed, to_east, to_west, to_north, to_south = block_table
    east_value, west_value, north_value, south_value = beside_all(padded)
    return (
        diagonal * grid_field
        + crossed * grid_field[::-1]
        - (
            to_east * east_value
            + to_west * west_value
            + to_north * north_value
            + to_south * south_value
        )
    )


def coarse_jacobi(block_table, right_side, widen_rim):
    answer = COARSE_WEIGHT * right_side / block_table[0]
    for sweep_at in range(CSWEEPS - 1):
        answer = (
            answer
            + COARSE_WEIGHT
            * (right_side - coarse_apply(block_table, answer, widen_rim(answer)))
            / block_table[0]
        )
    return answer


def least_squares(columns, initial_norm):
    steps_count = len(columns)
    matrix_rows = [
        [columns[column_at][row_at] for column_at in range(steps_count)]
        for row_at in range(steps_count + 1)
    ]
    target = [initial_norm] + [jnp.zeros_like(initial_norm) for row_at in range(steps_count)]
    for pivot_at in range(steps_count):
        top_value = matrix_rows[pivot_at][pivot_at]
        low_value = matrix_rows[pivot_at + 1][pivot_at]
        radius = jnp.sqrt(top_value * top_value + low_value * low_value)
        cosine = top_value / radius
        sine_value = low_value / radius
        for column_at in range(pivot_at, steps_count):
            upper_entry = matrix_rows[pivot_at][column_at]
            lower_entry = matrix_rows[pivot_at + 1][column_at]
            matrix_rows[pivot_at][column_at] = cosine * upper_entry + sine_value * lower_entry
            matrix_rows[pivot_at + 1][column_at] = cosine * lower_entry - sine_value * upper_entry
        upper_entry = target[pivot_at]
        lower_entry = target[pivot_at + 1]
        target[pivot_at] = cosine * upper_entry + sine_value * lower_entry
        target[pivot_at + 1] = cosine * lower_entry - sine_value * upper_entry
    weights = [None] * steps_count
    for pivot_at in reversed(range(steps_count)):
        partial_sum = target[pivot_at]
        for column_at in range(pivot_at + 1, steps_count):
            partial_sum = partial_sum - matrix_rows[pivot_at][column_at] * weights[column_at]
        weights[pivot_at] = partial_sum / matrix_rows[pivot_at][pivot_at]
    return weights


def body(forcing, viscosity, spread, coupling, friction, ice_mask, aggregates):
    layer_count = forcing.shape[1]
    ice_float = ice_mask.astype(jnp.float32)
    mask_padded = extended(ice_mask, (("gx", 0), ("gy", 1)), 1).astype(jnp.float32)
    fine_coefs = fine_coefficients(viscosity, spread, coupling, friction, ice_float, mask_padded)
    middle = group_layers(fine_coefs, 2)
    stencils = [fine_coefs, middle, group_layers(middle, layer_count // 2)]
    factors = [line_factor(level_coefs) for level_coefs in stencils]
    group_count = aggregates.shape[0] * aggregates.shape[1] // 16
    ids_flat = aggregates.reshape(-1)
    point_diag = point_diagonal(stencils[2], aggregates, group_count)
    block_table = coarse_coefficients(stencils[2], 1, 1)

    def fine_apply(grid_field):
        padded = extended(grid_field, (("gx", 2), ("gy", 3)), 1)
        return apply_stencil(stencils[0], grid_field, padded)

    def restrict_points(grid_field):
        flattened = grid_field.reshape(2, -1)
        return jnp.stack(
            [
                jax.ops.segment_sum(flattened[0], ids_flat, num_segments=group_count),
                jax.ops.segment_sum(flattened[1], ids_flat, num_segments=group_count),
            ]
        )

    def prolong_points(values):
        return values[:, ids_flat].reshape((2, 1) + aggregates.shape)

    def point_apply(values):
        prolonged = prolong_points(values)
        padded = extended(prolonged, (("gx", 2), ("gy", 3)), 1)
        return restrict_points(apply_stencil(stencils[2], prolonged, padded))

    def neighbour_widen(values):
        return extended(values, (("gx", 1), ("gy", 2)), 1)

    def coarse_correction(values):
        coarse_rhs = jnp.sum(values, axis=1).reshape(2, 1, 1)
        answer = coarse_jacobi(block_table, coarse_rhs, neighbour_widen)
        return answer.reshape(2, 1)

    def point_cycle(right_side):
        answer = POINT_WEIGHT * right_side / point_diag
        answer = answer + POINT_WEIGHT * (right_side - point_apply(answer)) / point_diag
        answer = answer + coarse_correction(right_side - point_apply(answer))
        for sweep_at in range(SWEEPS):
            answer = answer + POINT_WEIGHT * (right_side - point_apply(answer)) / point_diag
        return answer

    def descend(level_number, leftover):
        if level_number == 0:
            return expand_layers(line_cycle(1, group_sum(leftover, 2)), 2)
        if level_number == 1:
            depth_count = leftover.shape[1]
            return expand_layers(line_cycle(2, group_sum(leftover, depth_count)), depth_count)
        return prolong_points(point_cycle(restrict_points(leftover)))

    def sweep_apply(level_number, grid_field):
        if level_number == 0:
            padded = extended(grid_field, (("gx", 2), ("gy", 3)), 1)
        elif level_number == 1:
            padded = extended(grid_field, (("gx", 2), ("gy", 3)), 1)
        else:
            padded = extended(grid_field, (("gx", 2), ("gy", 3)), 1)
        return apply_stencil(stencils[level_number], grid_field, padded)

    def line_cycle(level_number, right_side):
        factor = factors[level_number]
        answer = LINE_WEIGHT * line_solve(factor, right_side)
        answer = answer + LINE_WEIGHT * line_solve(
            factor, right_side - sweep_apply(level_number, answer)
        )
        answer = answer + descend(level_number, right_side - sweep_apply(level_number, answer))
        for sweep_at in range(SWEEPS):
            answer = answer + LINE_WEIGHT * line_solve(
                factor, right_side - sweep_apply(level_number, answer)
            )
        return answer

    initial_norm = jnp.sqrt(lax.psum(jnp.sum(forcing * forcing), ("gx", "gy")))
    basis = [forcing / initial_norm]
    stored = []
    columns = []
    for step_at in range(ITERS):
        search = line_cycle(0, basis[step_at])
        stored.append(search)
        image = fine_apply(search)
        local_dots = jnp.stack([jnp.sum(vector * image) for vector in basis])
        projected, square_sum = lax.psum((local_dots, jnp.sum(image * image)), ("gx", "gy"))
        for index_at in range(len(basis)):
            image = image - projected[index_at] * basis[index_at]
        height = jnp.sqrt(square_sum - jnp.sum(projected * projected))
        columns.append(
            [projected[index_at] for index_at in range(len(basis))]
            + [height]
            + [jnp.zeros_like(height) for row_at in range(ITERS - 1 - step_at)]
        )
        if step_at + 1 < ITERS:
            basis.append(image / height)
    weights = least_squares(columns, initial_norm)
    solution = weights[0] * stored[0]
    for index_at in range(1, ITERS):
        solution = solution + weights[index_at] * stored[index_at]
    residual = forcing - fine_apply(solution)
    return (solution, residual)


def solution(mesh):
    return jax.shard_map(
        body,
        mesh=mesh,
        in_specs=(
            P(None, None, "gx", "gy"),
            P(None, "gx", "gy"),
            P(None, "gx", "gy"),
            P("gx", "gy"),
            P("gx", "gy"),
            P("gx", "gy"),
            P("gx", "gy"),
        ),
        out_specs=(P(None, None, "gx", "gy"), P(None, None, "gx", "gy")),
        check_vma=False,
    )
```

profile of v0, /device:TPU:0, one launch (start us, length us, event | category | flops | bytes accessed | tf_op | source)
XLA Modules:
  0.0 2252.2 jit_solution(12265902826835605389)
XLA Ops:
  8.1 42.2 %psum.49 = f32[]{:T(128)} all-reduce(f32[]{:T(128)} %multiply_reduce_fusion.9), channel_id=1, replica_groups=mesh['gx'=4,'gy'=8] {'gx','gy'}, use_global_device_ids=true, to_apply=%region_1.2 | all-reduce | flops 1 | bytes 8 | tf_op jit(solution)/shard_map/psum | solution.py:327
  88.1 20.5 collective-permute-done.7
  122.0 20.3 collective-permute-done.11
  236.0 14.9 scatter_custom_fusion.1
  640.7 18.1 collective-permute-done.75
  674.1 17.9 collective-permute-done.79
  726.4 48.6 %all-reduce.63 = (f32[]{:T(128)}, f32[1]{0:T(128)}) all-reduce(f32[]{:T(128)} %get-tuple-element.10, f32[1]{0:T(128)} %bitcast.151), channel_id=1, replica_groups=mesh['gx'=4,'gy'=8] {'gx','gy'}, use_global_device_ids=true, to_apply=%region_42.43 | all-reduce | flops 2 | bytes 16 | tf_op jit(solution)/shard_map/psum | solution.py:336
  790.3 20.2 collective-permute-done.87
  824.0 20.2 collective-permute-done.91
  941.7 14.8 scatter_custom_fusion.11
  981.3 14.8 scatter_custom_fusion.14
  1035.9 14.8 scatter_custom_fusion.16
  1148.3 14.8 scatter_custom_fusion.18
  1328.7 18.1 collective-permute-done.155
  1362.3 17.9 collective-permute-done.159
  1416.7 48.5 %all-reduce.62 = (f32[]{:T(128)}, f32[2]{0:T(128)S(1)}) all-reduce(f32[]{:T(128)} %get-tuple-element.7, f32[2]{0:T(128)S(1)} %pad_maximum_fusion.480), channel_id=1, replica_groups=mesh['gx'=4,'gy'=8] {'gx','gy'}, use_global_device_ids=true, to_apply=%region_60.61 | all-reduce | flops 3 | bytes 24 | tf_op jit(solution)/shard_map/psum | solution.py:336
  1482.7 20.2 collective-permute-done.167
  1516.7 20.2 collective-permute-done.171
  1623.5 15.4 scatter_custom_fusion.22
  1638.9 15.4 scatter_custom_fusion.21
  1685.3 15.3 scatter_custom_fusion.24
  1700.6 15.4 scatter_custom_fusion.23
  1747.8 15.3 scatter_custom_fusion.26
  1763.1 15.3 scatter_custom_fusion.25
  1875.5 15.4 scatter_custom_fusion.28
  1890.9 15.3 scatter_custom_fusion.27
  1938.3 15.3 scatter_custom_fusion.30
  1953.6 15.3 scatter_custom_fusion.29
  2071.7 18.1 collective-permute-done.235
  2105.8 17.7 collective-permute-done.239
  2164.2 48.5 %all-reduce.61 = (f32[3]{0:T(128)S(1)}, f32[]{:T(128)}) all-reduce(f32[3]{0:T(128)S(1)} %pad_maximum_fusion.481, f32[]{:T(128)} %get-tuple-element.2), channel_id=1, replica_groups=mesh['gx'=4,'gy'=8] {'gx','gy'}, use_global_device_ids=true, to_apply=%region_78.79 | all-reduce | flops 4 | bytes 32 | tf_op jit(solution)/shard_map/psum | solution.py:336
  2230.4 20.1 collective-permute-done.247
  (1701 shorter events, 1560.6 us)
Async XLA Ops:
  1.4 51.3 %collective-permute-start.1 = (s32[1,128]{1,0:T(1,128)S(1)}, s32[1,128]{1,0:T(1,128)S(1)}, u32[]{:S(2)}, u32[]{:S(2)}) collective-permute-start(s32[1,128]{1,0:T(1,128)S(1)} %get-tuple-element.789), channel_id=1, source_target_pairs={{8,0},{16,8},{24,16},{9,1},{17,9},{25,17},{10,2},{18,10},{26,18},{... | collective-permute-start | bytes 1544 | tf_op jit(solution)/shard_map/ppermute | solution.py:26
  2.7 50.0 %collective-permute-start = (s32[1,128]{1,0:T(1,128)S(1)}, s32[1,128]{1,0:T(1,128)S(1)}, u32[]{:S(2)}, u32[]{:S(2)}) collective-permute-start(s32[1,128]{1,0:T(1,128)S(1)} %get-tuple-element.788), channel_id=1, source_target_pairs={{0,8},{8,16},{16,24},{1,9},{9,17},{17,25},{2,10},{10,18},{18,26},{... | collective-permute-start | bytes 1544 | tf_op jit(solution)/shard_map/ppermute | solution.py:24
  81.8 26.8 %collective-permute-start.7 = (f32[2,20,18,1]{3,2,1,0:T(8,128)S(1)}, f32[2,20,18,1]{3,2,1,0:T(8,128)S(1)}, u32[]{:S(2)}, u32[]{:S(2)}) collective-permute-start(f32[2,20,18,1]{3,2,1,0:T(8,128)S(1)} %get-tuple-element.449), channel_id=1, source_target_pairs={{0,1},{1,2},{2,3},{3,4},{4,5},{5,6},{6,7},{8,9},{9,10},{10,11},{11... | collective-permute-start | bytes 8648 | tf_op jit(solution)/shard_map/ppermute | solution.py:24
  86.7 21.9 collective-permute-start.6
  116.2 26.1 %collective-permute-start.11 = (f32[2,20,18,1]{3,2,1,0:T(8,128)S(1)}, f32[2,20,18,1]{3,2,1,0:T(8,128)S(1)}, u32[]{:S(2)}, u32[]{:S(2)}) collective-permute-start(f32[2,20,18,1]{3,2,1,0:T(8,128)S(1)} %get-tuple-element.447), channel_id=1, source_target_pairs={{0,1},{1,2},{2,3},{3,4},{4,5},{5,6},{6,7},{8,9},{9,10},{10,11},{11... | collective-permute-start | bytes 8648 | tf_op jit(solution)/shard_map/ppermute | solution.py:24
  120.6 21.7 collective-permute-start.10
  214.8 21.1 collective-permute-start.27
  635.2 23.6 %collective-permute-start.75 = (f32[2,20,18,1]{3,2,1,0:T(8,128)S(1)}, f32[2,20,18,1]{3,2,1,0:T(8,128)S(1)}, u32[]{:S(2)}, u32[]{:S(2)}) collective-permute-start(f32[2,20,18,1]{3,2,1,0:T(8,128)S(1)} %get-tuple-element.445), channel_id=1, source_target_pairs={{0,1},{1,2},{2,3},{3,4},{4,5},{5,6},{6,7},{8,9},{9,10},{10,11},{11... | collective-permute-start | bytes 8648 | tf_op jit(solution)/shard_map/ppermute | solution.py:24
  639.3 19.5 collective-permute-start.74
  668.6 23.4 %collective-permute-start.79 = (f32[2,20,18,1]{3,2,1,0:T(8,128)S(1)}, f32[2,20,18,1]{3,2,1,0:T(8,128)S(1)}, u32[]{:S(2)}, u32[]{:S(2)}) collective-permute-start(f32[2,20,18,1]{3,2,1,0:T(8,128)S(1)} %get-tuple-element.443), channel_id=1, source_target_pairs={{0,1},{1,2},{2,3},{3,4},{4,5},{5,6},{6,7},{8,9},{9,10},{10,11},{11... | collective-permute-start | bytes 8648 | tf_op jit(solution)/shard_map/ppermute | solution.py:24
  672.7 19.3 collective-permute-start.78
  706.1 19.2 collective-permute-start.82
  784.6 26.0 %collective-permute-start.87 = (f32[2,20,18,1]{3,2,1,0:T(8,128)S(1)}, f32[2,20,18,1]{3,2,1,0:T(8,128)S(1)}, u32[]{:S(2)}, u32[]{:S(2)}) collective-permute-start(f32[2,20,18,1]{3,2,1,0:T(8,128)S(1)} %get-tuple-element.439), channel_id=1, source_target_pairs={{0,1},{1,2},{2,3},{3,4},{4,5},{5,6},{6,7},{8,9},{9,10},{10,11},{11... | collective-permute-start | bytes 8648 | tf_op jit(solution)/shard_map/ppermute | solution.py:24
  788.8 21.7 collective-permute-start.86
  818.2 26.0 %collective-permute-start.91 = (f32[2,20,18,1]{3,2,1,0:T(8,128)S(1)}, f32[2,20,18,1]{3,2,1,0:T(8,128)S(1)}, u32[]{:S(2)}, u32[]{:S(2)}) collective-permute-start(f32[2,20,18,1]{3,2,1,0:T(8,128)S(1)} %get-tuple-element.437), channel_id=1, source_target_pairs={{0,1},{1,2},{2,3},{3,4},{4,5},{5,6},{6,7},{8,9},{9,10},{10,11},{11... | collective-permute-start | bytes 8648 | tf_op jit(solution)/shard_map/ppermute | solution.py:24
  822.7 21.6 collective-permute-start.90
  1323.2 23.6 %collective-permute-start.155 = (f32[2,20,18,1]{3,2,1,0:T(8,128)S(1)}, f32[2,20,18,1]{3,2,1,0:T(8,128)S(1)}, u32[]{:S(2)}, u32[]{:S(2)}) collective-permute-start(f32[2,20,18,1]{3,2,1,0:T(8,128)S(1)} %get-tuple-element.435), channel_id=1, source_target_pairs={{0,1},{1,2},{2,3},{3,4},{4,5},{5,6},{6,7},{8,9},{9,10},{10,11},{11... | collective-permute-start | bytes 8648 | tf_op jit(solution)/shard_map/ppermute | solution.py:24
  1327.3 19.5 collective-permute-start.154
  1356.8 23.4 %collective-permute-start.159 = (f32[2,20,18,1]{3,2,1,0:T(8,128)S(1)}, f32[2,20,18,1]{3,2,1,0:T(8,128)S(1)}, u32[]{:S(2)}, u32[]{:S(2)}) collective-permute-start(f32[2,20,18,1]{3,2,1,0:T(8,128)S(1)} %get-tuple-element.433), channel_id=1, source_target_pairs={{0,1},{1,2},{2,3},{3,4},{4,5},{5,6},{6,7},{8,9},{9,10},{10,11},{11... | collective-permute-start | bytes 8648 | tf_op jit(solution)/shard_map/ppermute | solution.py:24
  1361.0 19.3 collective-permute-start.158
  1394.3 19.2 collective-permute-start.162
  1477.0 26.0 %collective-permute-start.167 = (f32[2,20,18,1]{3,2,1,0:T(8,128)S(1)}, f32[2,20,18,1]{3,2,1,0:T(8,128)S(1)}, u32[]{:S(2)}, u32[]{:S(2)}) collective-permute-start(f32[2,20,18,1]{3,2,1,0:T(8,128)S(1)} %get-tuple-element.429), channel_id=1, source_target_pairs={{0,1},{1,2},{2,3},{3,4},{4,5},{5,6},{6,7},{8,9},{9,10},{10,11},{11... | collective-permute-start | bytes 8648 | tf_op jit(solution)/shard_map/ppermute | solution.py:24
  1481.2 21.7 collective-permute-start.166
  1510.9 26.0 %collective-permute-start.171 = (f32[2,20,18,1]{3,2,1,0:T(8,128)S(1)}, f32[2,20,18,1]{3,2,1,0:T(8,128)S(1)}, u32[]{:S(2)}, u32[]{:S(2)}) collective-permute-start(f32[2,20,18,1]{3,2,1,0:T(8,128)S(1)} %get-tuple-element.427), channel_id=1, source_target_pairs={{0,1},{1,2},{2,3},{3,4},{4,5},{5,6},{6,7},{8,9},{9,10},{10,11},{11... | collective-permute-start | bytes 8648 | tf_op jit(solution)/shard_map/ppermute | solution.py:24
  1515.3 21.6 collective-permute-start.170
  2066.2 23.6 %collective-permute-start.235 = (f32[2,20,18,1]{3,2,1,0:T(8,128)S(1)}, f32[2,20,18,1]{3,2,1,0:T(8,128)S(1)}, u32[]{:S(2)}, u32[]{:S(2)}) collective-permute-start(f32[2,20,18,1]{3,2,1,0:T(8,128)S(1)} %get-tuple-element.425), channel_id=1, source_target_pairs={{0,1},{1,2},{2,3},{3,4},{4,5},{5,6},{6,7},{8,9},{9,10},{10,11},{11... | collective-permute-start | bytes 8648 | tf_op jit(solution)/shard_map/ppermute | solution.py:24
  2070.3 19.5 collective-permute-start.234
  2100.1 23.4 %collective-permute-start.239 = (f32[2,20,18,1]{3,2,1,0:T(8,128)S(1)}, f32[2,20,18,1]{3,2,1,0:T(8,128)S(1)}, u32[]{:S(2)}, u32[]{:S(2)}) collective-permute-start(f32[2,20,18,1]{3,2,1,0:T(8,128)S(1)} %get-tuple-element.423), channel_id=1, source_target_pairs={{0,1},{1,2},{2,3},{3,4},{4,5},{5,6},{6,7},{8,9},{9,10},{10,11},{11... | collective-permute-start | bytes 8648 | tf_op jit(solution)/shard_map/ppermute | solution.py:24
  2104.2 19.3 collective-permute-start.238
  2141.8 19.2 collective-permute-start.242
  2224.8 25.7 %collective-permute-start.247 = (f32[2,20,18,1]{3,2,1,0:T(8,128)S(1)}, f32[2,20,18,1]{3,2,1,0:T(8,128)S(1)}, u32[]{:S(2)}, u32[]{:S(2)}) collective-permute-start(f32[2,20,18,1]{3,2,1,0:T(8,128)S(1)} %get-tuple-element.419), channel_id=1, source_target_pairs={{0,1},{1,2},{2,3},{3,4},{4,5},{5,6},{6,7},{8,9},{9,10},{10,11},{11... | collective-permute-start | bytes 8648 | tf_op jit(solution)/shard_map/ppermute | solution.py:24
  2229.1 21.5 collective-permute-start.246
  (414 other events, 44763.5 us)
where the time goes:
time: 2270 us; the launch traced here: 2250 us
  starting transfers between devices  667 us (29%)
  waiting for transfers between devices  592 us (26%)
  other arithmetic  589 us (26%)
  local copies, waits for them, and re-layouts  190 us (8%)
  blocking collectives  188 us (8%)
  between operations  26.5 us (1%)
    ppermute x124, starting transfers between devices, extended(): lax.ppermute(tail, axis, [(i, (i + 1) % count) for i in range(ends)])  506 us
    ppermute x124, waiting for transfers between devices, extended(): lax.ppermute(tail, axis, [(i, (i + 1) % count) for i in range(ends)])  360 us
    ppermute x124, waiting for transfers between devices, extended(): lax.ppermute(head, axis, [((i + 1) % count, i) for i in range(ends)])  233 us
    scatter-add x15, other arithmetic, restrict_points(): jax.ops.segment_sum(flattened[1], ids_flat, num_segments=group_count)  224 us
    scatter-add x15, other arithmetic, restrict_points(): jax.ops.segment_sum(flattened[0], ids_flat, num_segments=group_count)  224 us
    ppermute x124, starting transfers between devices, extended(): lax.ppermute(head, axis, [((i + 1) % count, i) for i in range(ends)])  161 us
    psum x3, blocking collectives, body(): lax.psum((local_dots, jnp.sum(image * image)), ('gx', 'gy'))  146 us
    gather x15, local copies, waits for them, and re-layouts, prolong_points(): return values[:, ids_flat].reshape((2, 1) + aggregates.shape)  122 us
  transfers between devices with their start and end apart: 248, of which 149 were waited for; matrix products, arithmetic and copies ran while one was open for 1% of the time, Pallas kernels for 0%

commit v1 on v0

v1 whole, which is shorter than its diff:
```python
import jax
import jax.numpy as jnp
from jax import lax
from jax.experimental import pallas as pl
from jax.experimental.pallas import tpu as pltpu
from jax.sharding import PartitionSpec as P

ITERS = 3
CSWEEPS = 4
LINE_WEIGHT = 0.8
POINT_WEIGHT = 0.7
COARSE_WEIGHT = 0.7
MESH = pl.DeviceIdType.MESH
F32 = jnp.float32
BF16 = jnp.bfloat16
TOP = 8


def split(x):
    high = x.astype(BF16)
    return high, (x - high.astype(F32)).astype(BF16)


def dot(a, b, ca, cb):
    return lax.dot_general(a, b, (((ca,), (cb,)), ((), ())), preferred_element_type=F32)


def total(x):
    return jnp.sum(jnp.sum(x, axis=1, keepdims=True), axis=0, keepdims=True)


def kernel(nx, ny, layers, cx, cy, forcing, viscosity, spread, coupling, friction, mask, aggs,
           solution, residual, *scratch):
    count = nx * ny
    gx = lax.axis_index("gx")
    gy = lax.axis_index("gy")
    me = gx * ny + gy
    (levels, (basis, stored, images), (hit, big_hi, big_lo, point_diag, point_cross),
     (x_out, x_in, x_send, x_recv), gathers, heights) = scratch
    lane = lax.broadcasted_iota(jnp.int32, (cx, cy), 1)
    row = lax.broadcasted_iota(jnp.int32, (cx, cy), 0)
    first_lane, last_lane, even = lane == 0, lane == cy - 1, lane % 2 == 0
    pair = lane // 2
    own = pl.ds(TOP, cx)

    sides = (
        (gx < nx - 1, (gx + 1, gy)),
        (gx > 0, (gx - 1, gy)),
        (gy < ny - 1, (gx, gy + 1)),
        (gy > 0, (gx, gy - 1)),
    )

    def swap_edges(copies):
        for d in range(4):
            pl.when(sides[d][0])(copies[d].start)
        for d in range(4):
            @pl.when(sides[d][0])
            def _():
                copies[d].wait_send()
                copies[d ^ 1].wait_recv()

    class Level:
        def __init__(self, depth, refs):
            self.depth = depth
            (self.field, self.row_out, self.row_in, self.col_out, self.col_in, self.send, self.recv,
             self.diag, self.vert, self.side, self.cross, self.inverse, self.upper,
             self.right, self.forward, self.post) = refs

        def put(self, p, k, value, packed):
            self.field[p, k, :, own, :] = value
            self.row_out[p, 0, k] = value[:, cx - 1, :]
            self.row_out[p, 1, k] = value[:, 0, :]
            for v in range(2):
                m = 2 * k + v
                packed = jnp.where(pair == m, pltpu.roll(value[v], (2 * m + 1) % cy, 1), packed)
            return packed

        def exchange(self, p, packed):
            self.col_out[p] = packed
            copies = []
            for d in range(4):
                src = self.row_out.at[p, d] if d < 2 else self.col_out.at[p]
                dst = self.row_in.at[p, d] if d < 2 else self.col_in.at[p, d - 2]
                copies.append(pltpu.make_async_remote_copy(
                    src_ref=src, dst_ref=dst, send_sem=self.send.at[p, d],
                    recv_sem=self.recv.at[p, d ^ 1], device_id=sides[d][1], device_id_type=MESH))
            swap_edges(copies)
            for k in range(self.depth):
                self.field[p, k, :, TOP - 1, :] = self.row_in[p, 0, k]
                self.field[p, k, :, TOP + cx, :] = self.row_in[p, 1, k]
            return jnp.where(even, pltpu.roll(self.col_in[p, 1], cy - 1, 1),
                             pltpu.roll(self.col_in[p, 0], 1, 1))

        def beside(self, p, k, comb):
            value = self.field[p, k, :, own, :]
            north, south = [], []
            for v in range(2):
                edge = pltpu.roll(comb, (cy - 1 - 2 * (2 * k + v)) % cy, 1)
                north.append(jnp.where(last_lane, edge, pltpu.roll(value[v], cy - 1, 1)))
                south.append(jnp.where(first_lane, edge, pltpu.roll(value[v], 1, 1)))
            return (value, self.field[p, k, :, pl.ds(TOP + 1, cx), :],
                    self.field[p, k, :, pl.ds(TOP - 1, cx), :], jnp.stack(north), jnp.stack(south))

        def sideways(self, p, k, comb):
            value, east, west, north, south = self.beside(p, k, comb)
            out = (self.side[0, k][None] * east + self.side[1, k][None] * west
                   + self.side[2, k][None] * north + self.side[3, k][None] * south)
            if k == 0:
                crossed = self.cross[...]
                out = out - jnp.stack([crossed * value[1], crossed * value[0]])
            return value, out

        def leftover(self, p, comb, right, emit):
            for k in range(self.depth):
                value, out = self.sideways(p, k, comb)
                out = out - self.diag[k][None] * value
                if k + 1 < self.depth:
                    out = out + self.vert[k][None] * self.field[p, k + 1, :, own, :]
                if k > 0:
                    out = out + self.vert[k - 1][None] * self.field[p, k - 1, :, own, :]
                emit(k, out if right is None else right(k) + out)

        def solve(self, source, old, p):
            last = None
            for k in range(self.depth):
                value = source(k)
                if k > 0:
                    value = value + self.vert[k - 1][None] * last
                last = value * self.inverse[k][None]
                self.forward[k] = last
            packed = jnp.zeros((cx, cy), F32)
            for k in reversed(range(self.depth)):
                if k + 1 < self.depth:
                    last = self.forward[k] - self.upper[k][None] * last
                value = LINE_WEIGHT * last
                if old is not None:
                    value = value + (1.0 - LINE_WEIGHT) * old(k)
                packed = self.put(p, k, value, packed)
            return packed

        def sweep(self, p, comb, right):
            return self.solve(lambda k: right(k) + self.sideways(p, k, comb)[1],
                              lambda k: self.field[p, k, :, own, :], 1 - p)

        def factor(self):
            inverse = 1.0 / self.diag[0]
            self.inverse[0] = inverse
            for k in range(1, self.depth):
                ratio = -self.vert[k - 1] * inverse
                self.upper[k - 1] = ratio
                inverse = 1.0 / (self.diag[k] + self.vert[k - 1] * ratio)
                self.inverse[k] = inverse

        def cycle(self, right, inner):
            packed = self.solve(right, None, 0)
            comb = self.exchange(0, packed)
            packed = self.sweep(0, comb, right)
            comb = self.exchange(1, packed)
            correction = inner(self, 1, comb, right)
            packed = jnp.zeros((cx, cy), F32)
            for k in range(self.depth):
                packed = self.put(0, k, self.field[1, k, :, own, :] + correction(k), packed)
            comb = self.exchange(0, packed)
            packed = self.sweep(0, comb, right)
            comb = self.exchange(1, packed)
            return self.sweep(1, comb, right)

    half = layers // 2
    fine, middle, column = (Level(n, refs) for n, refs in zip((layers, half, 1), levels))
    for d in range(4):
        @pl.when(jnp.logical_not(sides[d][0]))
        def _():
            for level in (fine, middle, column):
                for p in range(2):
                    if d < 2:
                        level.row_in[p, d ^ 1] = jnp.zeros_like(level.row_in[p, d ^ 1])
                    else:
                        level.col_in[p, (d ^ 1) - 2] = jnp.zeros((cx, cy), F32)
            for p in range(2):
                x_in[p, d] = jnp.zeros((2, cy), F32)
    basis[...] = jnp.zeros_like(basis)

    def gather(which):
        out, into, send, recv = gathers[which]

        def step(i, carry):
            target = lax.rem(me + i, count)
            pltpu.make_async_remote_copy(
                src_ref=out, dst_ref=into.at[me], send_sem=send, recv_sem=recv,
                device_id=(target // ny, lax.rem(target, ny)), device_id_type=MESH).start()
            return carry

        lax.fori_loop(1, count, step, 0)
        into[me] = out[...]
        rest = into.at[pl.ds(0, count - 1)]
        pltpu.make_async_copy(rest, rest, recv).wait()
        pltpu.make_async_copy(rest, rest, send).wait()

    wide = lax.broadcasted_iota(jnp.int32, (1, cy), 1)

    def reduce_all(parts):
        line = jnp.zeros((1, cy), F32)
        for i, part in enumerate(parts):
            line = jnp.where(wide == i, part, line)
        gathers[1][0][...] = line
        gather(1)
        return jnp.sum(gathers[1][1][:, 0, :], axis=0, keepdims=True)

    def pick(line, i):
        return jnp.sum(jnp.where(wide == i, line, 0.0), axis=1, keepdims=True)

    ice = mask[...].astype(F32)
    ids = aggs[...]
    packed = column.put(1, 0, jnp.stack([ice, ids.astype(F32)]), jnp.zeros((cx, cy), F32))
    comb = column.exchange(1, packed)
    around = column.beside(1, 0, comb)[1:]
    bottom = friction[...]
    for k in range(layers):
        faces = 4.0 * spread[k]
        if k + 1 < layers:
            face = 0.5 * (viscosity[k] + viscosity[k + 1]) * ice
            fine.vert[k] = face
            faces = faces + face
        if k > 0:
            faces = faces + fine.vert[k - 1]
        if k == 0:
            faces = faces + bottom
        fine.diag[k] = ice * faces + (1.0 - ice)
        owned = spread[k] * ice
        for d in range(4):
            fine.side[d, k] = owned * around[d][0]
    fine.cross[...] = bottom * coupling[...] * ice
    for finer, coarser in ((fine, middle), (middle, column)):
        size = finer.depth // coarser.depth
        for k in range(coarser.depth):
            group = range(k * size, (k + 1) * size)
            diag = sum(finer.diag[j] for j in group)
            inner_faces = sum(finer.vert[j] for j in list(group)[:-1])
            coarser.diag[k] = diag - 2.0 * inner_faces
            if k + 1 < coarser.depth:
                coarser.vert[k] = finer.vert[group[-1]]
            for d in range(4):
                coarser.side[d, k] = sum(finer.side[d, j] for j in group)
        coarser.cross[...] = finer.cross[...]
    for level in (fine, middle, column):
        level.factor()

    down = lax.broadcasted_iota(jnp.int32, (cy, cy), 0)
    across = lax.broadcasted_iota(jnp.int32, (cy, cy), 1)
    for r in range(cx):
        hit[r] = jnp.where(ids[r:r + 1, :] == down, 1.0, 0.0).astype(BF16)
    side2 = [column.side[d, 0] for d in range(4)]
    diag2, cross2 = column.diag[0], column.cross[...]
    near = jnp.zeros((cy, cy), F32)
    for r in range(cx):
        here = hit[r].astype(F32)
        term = diag2[r:r + 1, :] * here
        if r + 1 < cx:
            term = term - side2[0][r:r + 1, :] * hit[r + 1].astype(F32)
        if r > 0:
            term = term - side2[1][r:r + 1, :] * hit[r - 1].astype(F32)
        term = term - jnp.where(across < cy - 1, side2[2][r:r + 1, :], 0.0) * pltpu.roll(here, cy - 1, 1)
        term = term - jnp.where(across > 0, side2[3][r:r + 1, :], 0.0) * pltpu.roll(here, 1, 1)
        high, low = split(term)
        near = near + dot(high, hit[r], 1, 1) + dot(low, hit[r], 1, 1)
    point_diag[...] = jnp.sum(jnp.where(down == across, near, 0.0), axis=0, keepdims=True)
    tables = [near]
    ids_around = [value[1] for value in around]
    for d, r in ((0, cx - 1), (1, 0)):
        other = ids_around[d][r:r + 1, :].astype(jnp.int32)
        term = jnp.where(other == down, side2[d][r:r + 1, :], 0.0)
        high, low = split(term)
        tables.append(-(dot(high, hit[r], 1, 1) + dot(low, hit[r], 1, 1)))
    for d, q in ((2, cy - 1), (3, 0)):
        other = ids_around[d][:, q:q + 1].astype(jnp.int32)
        term = jnp.where(other == lane, side2[d][:, q:q + 1], 0.0)
        here = jnp.where(ids[:, q:q + 1] == lane, 1.0, 0.0)
        high, low = split(term)
        here = here.astype(BF16)
        tables.append(-(dot(high, here, 0, 0) + dot(low, here, 0, 0)))
    for i, table in enumerate(tables):
        high, low = split(table)
        big_hi[i] = high
        big_lo[i] = low

    tall = lax.broadcasted_iota(jnp.int32, (4 * cx, cy), 0) % cx

    def restrict_points(first, second):
        h0, l0 = split(first)
        h1, l1 = split(second)
        left = jnp.concatenate([h0, h1, l0, l1], axis=0)
        out = jnp.zeros((4 * cx, cy), F32)
        for r in range(cx):
            out = jnp.where(tall == r, dot(left, hit[r], 1, 1), out)
        parts = [jnp.sum(out[i * cx:(i + 1) * cx] + out[(i + 2) * cx:(i + 3) * cx], axis=0, keepdims=True)
                 for i in range(2)]
        return jnp.concatenate(parts, axis=0)

    point_cross[...] = restrict_points(cross2, cross2)

    inner = (diag2 - jnp.where(row < cx - 1, side2[0], 0.0) - jnp.where(row > 0, side2[1], 0.0)
             - jnp.where(lane < cy - 1, side2[2], 0.0) - jnp.where(lane > 0, side2[3], 0.0))
    entries = (inner, cross2, jnp.where(row == cx - 1, side2[0], 0.0), jnp.where(row == 0, side2[1], 0.0),
               jnp.where(last_lane, side2[2], 0.0), jnp.where(first_lane, side2[3], 0.0))
    eight = lax.broadcasted_iota(jnp.int32, (8, cy), 0)
    tile = jnp.zeros((8, cy), F32)
    for i, entry in enumerate(entries):
        tile = jnp.where(eight == i, total(entry), tile)
    gathers[2][0][...] = tile
    gather(2)
    block_row = lax.broadcasted_iota(jnp.int32, (count, cy), 0)

    def coarse_correction(left):
        sums = jnp.sum(left, axis=1, keepdims=True)
        gathers[0][0][...] = jnp.where(wide % 2 == 0, sums[0:1], sums[1:2])
        gather(0)
        right = gathers[0][1][:, 0, :]
        diag, crossed, east, west, north, south = (gathers[2][1][:, i, :] for i in range(6))
        answer = COARSE_WEIGHT * right / diag
        for _ in range(CSWEEPS - 1):
            applied = diag * answer + crossed * pltpu.roll(answer, 1, 1) - (
                east * pltpu.roll(answer, count - ny, 0) + west * pltpu.roll(answer, ny, 0)
                + north * pltpu.roll(answer, count - 1, 0) + south * pltpu.roll(answer, 1, 0))
            answer = answer + COARSE_WEIGHT * (right - applied) / diag
        found = []
        for at in (me, me + ny, me - ny, me + 1, me - 1):
            line = jnp.sum(jnp.where(block_row == at, answer, 0.0), axis=0, keepdims=True)
            found.append(jnp.concatenate([line[:, 0:1], line[:, 1:2]], axis=0))
        return found

    def point_exchange(p, x):
        x_out[p] = x
        copies = [pltpu.make_async_remote_copy(
            src_ref=x_out.at[p], dst_ref=x_in.at[p, d ^ 1], send_sem=x_send.at[p, d],
            recv_sem=x_recv.at[p, d ^ 1], device_id=sides[d][1], device_id_type=MESH) for d in range(4)]
        swap_edges(copies)
        return [x] + [x_in[p, d] for d in range(4)]

    def point_apply(xs):
        out = point_cross[...] * jnp.concatenate([xs[0][1:2], xs[0][0:1]], axis=0)
        for i, x in enumerate(xs):
            high, low = split(x)
            out = out + dot(high, big_hi[i], 1, 0) + dot(low, big_hi[i], 1, 0) + dot(high, big_lo[i], 1, 0)
        return out

    def point_cycle(right):
        scale = POINT_WEIGHT / point_diag[...]
        x = right * scale
        x = x + (right - point_apply(point_exchange(0, x))) * scale
        xs = point_exchange(1, x)
        found = coarse_correction(right - point_apply(xs))
        xs = [x + y for x, y in zip(xs, found)]
        x = xs[0] + (right - point_apply(xs)) * scale
        return x + (right - point_apply(point_exchange(0, x))) * scale

    def into_points(level, p, comb, right):
        kept = []
        level.leftover(p, comb, right, lambda k, value: kept.append(value))
        x = point_cycle(restrict_points(kept[0][0], kept[0][1]))
        spread_out = jnp.stack([
            jnp.take_along_axis(jnp.broadcast_to(x[v:v + 1], (cx, cy)), ids, axis=1,
                                mode="promise_in_bounds") for v in range(2)])
        return lambda k: spread_out

    def into_level(coarser, deeper):
        def inner(level, p, comb, right):
            size = level.depth // coarser.depth
            held = []

            def emit(k, value):
                held.append(value)
                if len(held) == size:
                    coarser.right[k // size] = sum(held)
                    held.clear()

            level.leftover(p, comb, right, emit)
            coarser.cycle(lambda k: coarser.right[k], deeper)
            return lambda k: coarser.field[0, k // size, :, own, :]
        return inner

    into_column = into_level(column, into_points)
    into_middle = into_level(middle, into_column)

    square = jnp.zeros((cx, cy), F32)
    for k in range(layers):
        square = square + forcing[0, k] * forcing[0, k] + forcing[1, k] * forcing[1, k]
    norm = jnp.sqrt(pick(reduce_all([total(square)]), 0))
    for k in range(layers):
        basis[0, k] = forcing[:, k] / norm

    def iteration(j, carry):
        packed = fine.cycle(lambda k: basis[j, k], into_middle)
        comb = fine.exchange(0, packed)
        sums = [jnp.zeros((cx, cy), F32) for _ in range(ITERS + 1)]

        def emit(k, value):
            value = -value
            images[j, k] = value
            stored[j, k] = fine.field[0, k, :, own, :]
            for i in range(ITERS):
                prod = basis[i, k] * value
                sums[i] = sums[i] + prod[0] + prod[1]
            sums[ITERS] = sums[ITERS] + value[0] * value[0] + value[1] * value[1]

        fine.leftover(0, comb, None, emit)
        line = reduce_all([total(s) for s in sums])
        projected = [pick(line, i) for i in range(ITERS)]
        height2 = pick(line, ITERS)
        for h in projected:
            height2 = height2 - h * h
        height = jnp.sqrt(height2)
        heights[j] = jnp.where(wide == ITERS, height, line)

        @pl.when(j + 1 < ITERS)
        def _():
            for k in range(layers):
                value = images[j, k]
                for i in range(ITERS):
                    value = value - projected[i] * basis[i, k]
                basis[j + 1, k] = value / height
        return carry

    lax.fori_loop(0, ITERS, iteration, 0)

    rows = [[None] * ITERS for _ in range(ITERS + 1)]
    for j in range(ITERS):
        line = heights[j]
        for i in range(ITERS + 1):
            if i <= j:
                rows[i][j] = pick(line, i)
            elif i == j + 1:
                rows[i][j] = pick(line, ITERS)
            else:
                rows[i][j] = jnp.zeros((1, 1), F32)
    target = [norm] + [jnp.zeros((1, 1), F32)] * ITERS
    for a in range(ITERS):
        high, low = rows[a][a], rows[a + 1][a]
        radius = jnp.sqrt(high * high + low * low)
        cosine, sine = high / radius, low / radius
        for c in range(a, ITERS):
            up, lo = rows[a][c], rows[a + 1][c]
            rows[a][c] = cosine * up + sine * lo
            rows[a + 1][c] = cosine * lo - sine * up
        up, lo = target[a], target[a + 1]
        target[a] = cosine * up + sine * lo
        target[a + 1] = cosine * lo - sine * up
    weights = [None] * ITERS
    for a in reversed(range(ITERS)):
        part = target[a]
        for c in range(a + 1, ITERS):
            part = part - rows[a][c] * weights[c]
        weights[a] = part / rows[a][a]
    for k in range(layers):
        out = weights[0] * stored[0, k]
        rest = forcing[:, k] - weights[0] * images[0, k]
        for j in range(1, ITERS):
            out = out + weights[j] * stored[j, k]
            rest = rest - weights[j] * images[j, k]
        solution[:, k] = out
        residual[:, k] = rest


def solution(mesh):
    nx, ny = mesh.shape["gx"], mesh.shape["gy"]
    count = nx * ny

    def body(forcing, viscosity, spread, coupling, friction, mask, aggs):
        layers, cx, cy = forcing.shape[1:]
        dma = pltpu.SemaphoreType.DMA

        def vm(*shape, dtype=F32):
            return pltpu.VMEM(shape, dtype)

        def level(n):
            return (
                vm(2, n, 2, cx + 2 * TOP, cy), vm(2, 2, n, 2, cy), vm(2, 2, n, 2, cy),
                vm(2, cx, cy), vm(2, 2, cx, cy), dma((2, 4)), dma((2, 4)),
                vm(n, cx, cy), vm(n, cx, cy), vm(4, n, cx, cy), vm(cx, cy), vm(n, cx, cy), vm(n, cx, cy),
                vm(n, 2, cx, cy), vm(n, 2, cx, cy), vm(1, cy),
            )

        scratch = (
            (level(layers), level(layers // 2), level(1)),
            tuple(vm(ITERS, layers, 2, cx, cy) for _ in range(3)),
            (vm(cx, cy, cy, dtype=BF16), vm(5, cy, cy, dtype=BF16), vm(5, cy, cy, dtype=BF16),
             vm(1, cy), vm(2, cy)),
            (vm(2, 2, cy), vm(2, 4, 2, cy), dma((2, 4)), dma((2, 4))),
            tuple((vm(n, cy), vm(count, n, cy), dma(()), dma(())) for n in (1, 1, 8)),
            vm(ITERS, 1, cy),
        )
        flat, tree = jax.tree.flatten(scratch)

        def run(*refs):
            kernel(nx, ny, layers, cx, cy, *refs[:9], *jax.tree.unflatten(tree, refs[9:]))

        shape = jax.ShapeDtypeStruct(forcing.shape, F32)
        whole = pl.BlockSpec(memory_space=pltpu.VMEM)
        return tuple(pl.pallas_call(
            run,
            out_shape=(shape, shape),
            in_specs=[whole] * 7,
            out_specs=(whole, whole),
            scratch_shapes=flat,
            compiler_params=pltpu.CompilerParams(has_side_effects=True, vmem_limit_bytes=60 * 1024 * 1024),
        )(forcing, viscosity, spread, coupling, friction, mask, aggs))

    return jax.shard_map(
        body,
        mesh=mesh,
        in_specs=(
            P(None, None, "gx", "gy"),
            P(None, "gx", "gy"),
            P(None, "gx", "gy"),
            P("gx", "gy"),
            P("gx", "gy"),
            P("gx", "gy"),
            P("gx", "gy"),
        ),
        out_specs=(P(None, None, "gx", "gy"), P(None, None, "gx", "gy")),
        check_vma=False,
    )
```

time: 2270 us -> 228 us (0.10)
  starting transfers between devices: 667 us -> 0 us
  waiting for transfers between devices: 592 us -> 0 us
  other arithmetic: 589 us -> 0 us
  Pallas kernels: 0 us -> 225 us
  blocking collectives: 188 us -> 0 us
  local copies, waits for them, and re-layouts: 190 us -> 2.49 us
  between operations: 26.5 us -> 0.65 us
    ppermute x248 -> x0, starting transfers between devices: 667 us -> none  [the longest x124 506 us: extended(): lax.ppermute(tail, axis, [(i, (i + 1) % count) for i in range(ends)])]
    ppermute x248 -> x0, waiting for transfers between devices: 592 us -> none  [the longest x124 360 us: extended(): lax.ppermute(tail, axis, [(i, (i + 1) % count) for i in range(ends)])]
    scatter-add x31 -> x0, other arithmetic: 463 us -> none  [the longest x15 224 us: restrict_points(): jax.ops.segment_sum(flattened[1], ids_flat, num_segments=group_count)]
    pallas_call x0 -> x1, Pallas kernels: none -> 225 us  [body(): pl.pallas_call(run, out_shape=(shape, shape), in_specs=[whole] * 7, out_s...]
    psum x4 -> x0, blocking collectives: 188 us -> none  [the longest x3 146 us: body(): lax.psum((local_dots, jnp.sum(image * image)), ('gx', 'gy'))]
    gather x15 -> x0, local copies, waits for them, and re-layouts: 122 us -> none  [prolong_points(): return values[:, ids_flat].reshape((2, 1) + aggregates.shape)]
    add x58 -> x0, other arithmetic: 38.8 us -> none  [the longest x6 21.6 us: coarse_jacobi(): answer + COARSE_WEIGHT * (right_side - coarse_apply(block_table, answer,...]
    unnamed x180 -> x0, other arithmetic: 27.5 us -> none
  transfers between devices with their start and end apart: 248 -> 0, of which waited for: 149 -> 0; matrix products, arithmetic and copies ran while one was open for 1% -> 0% of each run, Pallas kernels for 0% -> 0%
where the time goes in v1:
time: 228 us
  Pallas kernels  225 us (99%)
  local copies, waits for them, and re-layouts  2.49 us (1%)
    pallas_call x1, Pallas kernels, body(): pl.pallas_call(run, out_shape=(shape, shape), in_specs=[whole] * 7, out_s...  225 us

profile of v1, /device:TPU:0, one launch (start us, length us, event | category | flops | bytes accessed | tf_op | source)
XLA Modules:
  0.0 228.2 jit_solution(12966972103115015841)
XLA Ops:
  0.6 225.0 %shard_map.86 = (f32[2,20,16,128]{3,2,1,0:T(8,128)}, f32[2,20,16,128]{3,2,1,0:T(8,128)}) custom-call(f32[2,20,16,128]{3,2,1,0:T(8,128)} %refs_0_.1, f32[20,16,128]{2,1,0:T(8,128)} %refs_1_.1, f32[20,16,128]{2,1,0:T(8,128)} %refs_2_.1, f32[16,128]{1,0:T(8,128)} %refs_3_.1, f32[16,128]{1,0:T(8,128)} %refs_4_.1, s32[16,128]{1,0:T(8,128)} %refs_5_.1, ...), custom_call_target="tpu_custom_call" | custom-call | tf_op jit(solution)/shard_map/pallas_call | solution.py:498
  225.7 0.0 copy-start
  225.7 1.8 copy.11
  227.5 0.0 copy-done
  227.5 0.7 copy.12
Async XLA Ops:
  225.7 1.8 copy-start

commit v2 on v1

--- a/solution.py
+++ b/solution.py
@@ -35,8 +35,8 @@
     gx = lax.axis_index("gx")
     gy = lax.axis_index("gy")
     me = gx * ny + gy
-    (levels, (basis, stored, images), (hit, big_hi, big_lo, point_diag, point_cross),
-     (x_out, x_in, x_send, x_recv), gathers, heights) = scratch
+    (levels, (basis, stored), (hit, big_hi, big_lo, point_diag, point_cross),
+     (x_out, x_in, x_send, x_recv), gathers) = scratch
     lane = lax.broadcasted_iota(jnp.int32, (cx, cy), 1)
     row = lax.broadcasted_iota(jnp.int32, (cx, cy), 0)
     first_lane, last_lane, even = lane == 0, lane == cy - 1, lane % 2 == 0
@@ -62,6 +62,7 @@
     class Level:
         def __init__(self, depth, refs):
             self.depth = depth
+            self.turn = 0
             (self.field, self.row_out, self.row_in, self.col_out, self.col_in, self.send, self.recv,
              self.diag, self.vert, self.side, self.cross, self.inverse, self.upper,
              self.right, self.forward, self.post) = refs
@@ -77,19 +78,20 @@
 
         def exchange(self, p, packed):
             self.col_out[p] = packed
+            q = lax.rem(p + self.turn, 2)
             copies = []
             for d in range(4):
                 src = self.row_out.at[p, d] if d < 2 else self.col_out.at[p]
-                dst = self.row_in.at[p, d] if d < 2 else self.col_in.at[p, d - 2]
+                dst = self.row_in.at[q, d] if d < 2 else self.col_in.at[q, d - 2]
                 copies.append(pltpu.make_async_remote_copy(
                     src_ref=src, dst_ref=dst, send_sem=self.send.at[p, d],
-                    recv_sem=self.recv.at[p, d ^ 1], device_id=sides[d][1], device_id_type=MESH))
+                    recv_sem=self.recv.at[q, d ^ 1], device_id=sides[d][1], device_id_type=MESH))
             swap_edges(copies)
             for k in range(self.depth):
-                self.field[p, k, :, TOP - 1, :] = self.row_in[p, 0, k]
-                self.field[p, k, :, TOP + cx, :] = self.row_in[p, 1, k]
-            return jnp.where(even, pltpu.roll(self.col_in[p, 1], cy - 1, 1),
-                             pltpu.roll(self.col_in[p, 0], 1, 1))
+                self.field[p, k, :, TOP - 1, :] = self.row_in[q, 0, k]
+                self.field[p, k, :, TOP + cx, :] = self.row_in[q, 1, k]
+            return jnp.where(even, pltpu.roll(self.col_in[q, 1], cy - 1, 1),
+                             pltpu.roll(self.col_in[q, 0], 1, 1))
 
         def beside(self, p, k, comb):
             value = self.field[p, k, :, own, :]
@@ -178,10 +180,10 @@
                         level.col_in[p, (d ^ 1) - 2] = jnp.zeros((cx, cy), F32)
             for p in range(2):
                 x_in[p, d] = jnp.zeros((2, cy), F32)
-    basis[...] = jnp.zeros_like(basis)
-
-    def gather(which):
+
+    def gather(which, slot=0):
         out, into, send, recv = gathers[which]
+        into, recv = into.at[slot], recv.at[slot]
 
         def step(i, carry):
             target = lax.rem(me + i, count)
@@ -204,7 +206,7 @@
             line = jnp.where(wide == i, part, line)
         gathers[1][0][...] = line
         gather(1)
-        return jnp.sum(gathers[1][1][:, 0, :], axis=0, keepdims=True)
+        return jnp.sum(gathers[1][1][0, :, 0, :], axis=0, keepdims=True)
 
     def pick(line, i):
         return jnp.sum(jnp.where(wide == i, line, 0.0), axis=1, keepdims=True)
@@ -313,9 +315,10 @@
     def coarse_correction(left):
         sums = jnp.sum(left, axis=1, keepdims=True)
         gathers[0][0][...] = jnp.where(wide % 2 == 0, sums[0:1], sums[1:2])
-        gather(0)
-        right = gathers[0][1][:, 0, :]
-        diag, crossed, east, west, north, south = (gathers[2][1][:, i, :] for i in range(6))
+        slot = lax.rem(fine.turn, 2)
+        gather(0, slot)
+        right = gathers[0][1][slot, :, 0, :]
+        diag, crossed, east, west, north, south = (gathers[2][1][0, :, i, :] for i in range(6))
         answer = COARSE_WEIGHT * right / diag
         for _ in range(CSWEEPS - 1):
             applied = diag * answer + crossed * pltpu.roll(answer, 1, 1) - (
@@ -330,11 +333,12 @@
 
     def point_exchange(p, x):
         x_out[p] = x
+        q = lax.rem(p + fine.turn, 2)
         copies = [pltpu.make_async_remote_copy(
-            src_ref=x_out.at[p], dst_ref=x_in.at[p, d ^ 1], send_sem=x_send.at[p, d],
-            recv_sem=x_recv.at[p, d ^ 1], device_id=sides[d][1], device_id_type=MESH) for d in range(4)]
+            src_ref=x_out.at[p], dst_ref=x_in.at[q, d ^ 1], send_sem=x_send.at[p, d],
+            recv_sem=x_recv.at[q, d ^ 1], device_id=sides[d][1], device_id_type=MESH) for d in range(4)]
         swap_edges(copies)
-        return [x] + [x_in[p, d] for d in range(4)]
+        return [x] + [x_in[q, d] for d in range(4)]
 
     def point_apply(xs):
         out = point_cross[...] * jnp.concatenate([xs[0][1:2], xs[0][0:1]], axis=0)
@@ -381,81 +385,51 @@
     into_column = into_level(column, into_points)
     into_middle = into_level(middle, into_column)
 
-    square = jnp.zeros((cx, cy), F32)
     for k in range(layers):
-        square = square + forcing[0, k] * forcing[0, k] + forcing[1, k] * forcing[1, k]
-    norm = jnp.sqrt(pick(reduce_all([total(square)]), 0))
-    for k in range(layers):
-        basis[0, k] = forcing[:, k] / norm
+        basis[0, k] = forcing[:, k]
 
     def iteration(j, carry):
+        fine.turn = j
         packed = fine.cycle(lambda k: basis[j, k], into_middle)
         comb = fine.exchange(0, packed)
-        sums = [jnp.zeros((cx, cy), F32) for _ in range(ITERS + 1)]
 
         def emit(k, value):
-            value = -value
-            images[j, k] = value
+            basis[j + 1, k] = value
             stored[j, k] = fine.field[0, k, :, own, :]
-            for i in range(ITERS):
-                prod = basis[i, k] * value
-                sums[i] = sums[i] + prod[0] + prod[1]
-            sums[ITERS] = sums[ITERS] + value[0] * value[0] + value[1] * value[1]
-
-        fine.leftover(0, comb, None, emit)
-        line = reduce_all([total(s) for s in sums])
-        projected = [pick(line, i) for i in range(ITERS)]
-        height2 = pick(line, ITERS)
-        for h in projected:
-            height2 = height2 - h * h
-        height = jnp.sqrt(height2)
-        heights[j] = jnp.where(wide == ITERS, height, line)
-
-        @pl.when(j + 1 < ITERS)
-        def _():
-            for k in range(layers):
-                value = images[j, k]
-                for i in range(ITERS):
-                    value = value - projected[i] * basis[i, k]
-                basis[j + 1, k] = value / height
+
+        fine.leftover(0, comb, lambda k: basis[j, k], emit)
         return carry
 
     lax.fori_loop(0, ITERS, iteration, 0)
 
-    rows = [[None] * ITERS for _ in range(ITERS + 1)]
-    for j in range(ITERS):
-        line = heights[j]
-        for i in range(ITERS + 1):
-            if i <= j:
-                rows[i][j] = pick(line, i)
-            elif i == j + 1:
-                rows[i][j] = pick(line, ITERS)
-            else:
-                rows[i][j] = jnp.zeros((1, 1), F32)
-    target = [norm] + [jnp.zeros((1, 1), F32)] * ITERS
+    names = [(i, j) for i in range(ITERS + 1) for j in range(i, ITERS + 1)]
+    sums = {name: jnp.zeros((cx, cy), F32) for name in names}
+    for k in range(layers):
+        chain = [basis[i, k] for i in range(ITERS + 1)]
+        terms = [chain[j] - chain[j + 1] for j in range(ITERS)] + [chain[0]]
+        for i, j in names:
+            prod = terms[i] * terms[j]
+            sums[i, j] = sums[i, j] + prod[0] + prod[1]
+    line = reduce_all([total(sums[name]) for name in names])
+    gram = {name: pick(line, at) for at, name in enumerate(names)}
+    rows = [[gram[min(i, j), max(i, j)] for j in range(ITERS + 1)] for i in range(ITERS)]
     for a in range(ITERS):
-        high, low = rows[a][a], rows[a + 1][a]
-        radius = jnp.sqrt(high * high + low * low)
-        cosine, sine = high / radius, low / radius
-        for c in range(a, ITERS):
-            up, lo = rows[a][c], rows[a + 1][c]
-            rows[a][c] = cosine * up + sine * lo
-            rows[a + 1][c] = cosine * lo - sine * up
-        up, lo = target[a], target[a + 1]
-        target[a] = cosine * up + sine * lo
-        target[a + 1] = cosine * lo - sine * up
+        for i in range(a + 1, ITERS):
+            share = rows[i][a] / rows[a][a]
+            for c in range(a, ITERS + 1):
+                rows[i][c] = rows[i][c] - share * rows[a][c]
     weights = [None] * ITERS
     for a in reversed(range(ITERS)):
-        part = target[a]
+        part = rows[a][ITERS]
         for c in range(a + 1, ITERS):
             part = part - rows[a][c] * weights[c]
         weights[a] = part / rows[a][a]
     for k in range(layers):
         out = weights[0] * stored[0, k]
-        rest = forcing[:, k] - weights[0] * images[0, k]
+        rest = forcing[:, k] - weights[0] * (basis[0, k] - basis[1, k])
         for j in range(1, ITERS):
             out = out + weights[j] * stored[j, k]
-            rest = rest - weights[j] * images[j, k]
+            rest = rest - weights[j] * (basis[j, k] - basis[j + 1, k])
         solution[:, k] = out
         residual[:, k] = rest
 
@@ -481,12 +455,11 @@
 
         scratch = (
             (level(layers), level(layers // 2), level(1)),
-            tuple(vm(ITERS, layers, 2, cx, cy) for _ in range(3)),
+            tuple(vm(n, layers, 2, cx, cy) for n in (ITERS + 1, ITERS)),
             (vm(cx, cy, cy, dtype=BF16), vm(5, cy, cy, dtype=BF16), vm(5, cy, cy, dtype=BF16),
              vm(1, cy), vm(2, cy)),
             (vm(2, 2, cy), vm(2, 4, 2, cy), dma((2, 4)), dma((2, 4))),
-            tuple((vm(n, cy), vm(count, n, cy), dma(()), dma(())) for n in (1, 1, 8)),
-            vm(ITERS, 1, cy),
+            tuple((vm(n, cy), vm(2, count, n, cy), dma(()), dma((2,))) for n in (1, 1, 8)),
         )
         flat, tree = jax.tree.flatten(scratch)
 

time: 228 us -> 214 us (0.939)
  Pallas kernels: 225 us -> 210 us
    pallas_call x1, Pallas kernels: 225 us -> 210 us  [body(): pl.pallas_call(run, out_shape=(shape, shape), in_specs=[whole] * 7, out_s...]
where the time goes in v2:
time: 214 us; the launch traced here: 213 us
  Pallas kernels  210 us (98%)
  local copies, waits for them, and re-layouts  2.49 us (1%)
    pallas_call x1, Pallas kernels, body(): pl.pallas_call(run, out_shape=(shape, shape), in_specs=[whole] * 7, out_s...  210 us

profile of v2, /device:TPU:0, one launch (start us, length us, event | category | flops | bytes accessed | tf_op | source)
XLA Modules:
  0.0 213.4 jit_solution(6759435410350086943)
XLA Ops:
  0.6 210.2 %shard_map.86 = (f32[2,20,16,128]{3,2,1,0:T(8,128)}, f32[2,20,16,128]{3,2,1,0:T(8,128)}) custom-call(f32[2,20,16,128]{3,2,1,0:T(8,128)} %refs_0_.1, f32[20,16,128]{2,1,0:T(8,128)} %refs_1_.1, f32[20,16,128]{2,1,0:T(8,128)} %refs_2_.1, f32[16,128]{1,0:T(8,128)} %refs_3_.1, f32[16,128]{1,0:T(8,128)} %refs_4_.1, s32[16,128]{1,0:T(8,128)} %refs_5_.1, ...), custom_call_target="tpu_custom_call" | custom-call | tf_op jit(solution)/shard_map/pallas_call | solution.py:471
  210.8 0.0 copy-start
  210.9 1.8 copy.11
  212.6 0.0 copy-done
  212.6 0.7 copy.12
Async XLA Ops:
  210.8 1.8 copy-start
